TPU v7x, 32 devices: a whole 2x2x4 slice. The times are simulated.
32 devices in a mesh: wide: 8 (over z, x), narrow: 4 (over y, core).
Axes of the slice: x: 2, y: 2, z: 4, core: 2. Of those that a mesh axis runs over, the one named last changes fastest.
Arguments:
- block_in: bfloat16 [160, 200, 768], P(('wide', 'narrow')), may hold values from -6 to 6
- out_grad: bfloat16 [160, 200, 768], P(('wide', 'narrow')), may hold values from -6 to 6
- mim_mask: int32 [160, 200], P(('wide', 'narrow')), may hold values from 0 to 1, as said below
- rel_index: int32 [200, 200], replicated, may hold values from 0 to 731
- qkv_weight: bfloat16 [768, 2304], replicated, may hold values from -0.21875 to 0.21875
- proj_weight: bfloat16 [768, 768], replicated, may hold values from -0.875 to 0.875
- up_weight: bfloat16 [768, 3072], P(None, 'narrow'), may hold values from -0.21875 to 0.21875
- down_weight: bfloat16 [768, 3072], P(None, 'narrow'), may hold values from -0.109375 to 0.109375
- vectors: float32 [10, 768], replicated
- up_bias: float32 [3072], replicated, may hold values from -1.5 to 1.5
- rel_table: float32 [732, 12], replicated, may hold values from -4 to 4
- qkv_master: float32 [768, 2304], P('wide', 'narrow'), may hold values from -0.21875 to 0.21875
- qkv_mean: float32 [768, 2304], P('wide', 'narrow'), may hold values from -0.00061035156 to 0.00061035156
- qkv_square: float32 [768, 2304], P('wide', 'narrow'), may hold values from 7.064254e-11 to 1.1302806e-09
- proj_master: float32 [768, 768], P('wide', 'narrow'), may hold values from -0.875 to 0.875
- proj_mean: float32 [768, 768], P('wide', 'narrow'), may hold values from -0.00061035156 to 0.00061035156
- proj_square: float32 [768, 768], P('wide', 'narrow'), may hold values from 7.064254e-11 to 1.1302806e-09
- up_master: float32 [768, 3072], P('wide', 'narrow'), may hold values from -0.21875 to 0.21875
- up_mean: float32 [768, 3072], P('wide', 'narrow'), may hold values from -0.00061035156 to 0.00061035156
- up_square: float32 [768, 3072], P('wide', 'narrow'), may hold values from 7.064254e-11 to 1.1302806e-09
- down_master: float32 [768, 3072], P('wide', 'narrow'), may hold values from -0.109375 to 0.109375
- down_mean: float32 [768, 3072], P('wide', 'narrow'), may hold values from -0.00061035156 to 0.00061035156
- down_square: float32 [768, 3072], P('wide', 'narrow'), may hold values from 7.064254e-11 to 1.1302806e-09
- vector_mean: float32 [10, 768], replicated, may hold values from -0.001953125 to 0.001953125
- vector_square: float32 [10, 768], replicated, may hold values from 6.3578287e-10 to 1.0172526e-08
- bias_mean: float32 [3072], replicated, may hold values from -0.001953125 to 0.001953125
- bias_square: float32 [3072], replicated, may hold values from 4.2385526e-11 to 1.695421e-10
- table_mean: float32 [732, 12], replicated, may hold values from -0.001953125 to 0.001953125
- table_square: float32 [732, 12], replicated, may hold values from 4.2385526e-11 to 1.695421e-10
Outputs:
- block_out: bfloat16 [160, 200, 768], P(('wide', 'narrow'))
- input_grad: float32 [160, 200, 768], P(('wide', 'narrow'))
- grad_norm: float32 [], replicated
- qkv_mean_new: float32 [768, 2304], P('wide', 'narrow')
- qkv_square_new: float32 [768, 2304], P('wide', 'narrow')
- qkv_new: float32 [768, 2304], P('wide', 'narrow')
- qkv_copy: bfloat16 [768, 2304], P('wide', 'narrow')
- proj_mean_new: float32 [768, 768], P('wide', 'narrow')
- proj_square_new: float32 [768, 768], P('wide', 'narrow')
- proj_new: float32 [768, 768], P('wide', 'narrow')
- proj_copy: bfloat16 [768, 768], P('wide', 'narrow')
- up_mean_new: float32 [768, 3072], P('wide', 'narrow')
- up_square_new: float32 [768, 3072], P('wide', 'narrow')
- up_new: float32 [768, 3072], P('wide', 'narrow')
- up_copy: bfloat16 [768, 3072], P('wide', 'narrow')
- down_mean_new: float32 [768, 3072], P('wide', 'narrow')
- down_square_new: float32 [768, 3072], P('wide', 'narrow')
- down_new: float32 [768, 3072], P('wide', 'narrow')
- down_copy: bfloat16 [768, 3072], P('wide', 'narrow')
- vector_mean_new: float32 [10, 768], replicated
- vector_square_new: float32 [10, 768], replicated
- vectors_new: float32 [10, 768], replicated
- bias_mean_new: float32 [3072], replicated
- bias_square_new: float32 [3072], replicated
- up_bias_new: float32 [3072], replicated
- table_mean_new: float32 [732, 12], replicated
- table_square_new: float32 [732, 12], replicated
- table_new: float32 [732, 12], replicated
Inputs may be any that keep to these rules, and one draw needn't show every extreme that they name: `mim_mask`: each image masks its own share of patches, from almost none to about three quarters, very unequal between images; position 0 and positions from 197 on are never masked.
All inputs are finite; a program needn't handle non-finite values.
Results may differ from a plain program's by a relative error of at most 0.012.
Values may be sent and summed in bfloat16 or wider, within the bound.
No kernel may reach another device: no remote copies, remote signals or barrier semaphores. Data moves between devices by JAX's collectives and lax.ppermute only.
A program may use at most 192 MiB of HBM per device.

v0:
```python
import jax
import jax.numpy as jnp
from jax import lax
from jax.sharding import PartitionSpec as P

VALID = 197
STEP = 10
norm_eps = 1e-06
clip_eps = 1e-06
max_norm = 1.0
beta_one = 0.9
beta_two = 0.999
adam_eps = 1e-08
rate_matrix = 0.05
rate_small = 0.4
weight_decay = 0.05
exact_prec = lax.Precision.HIGHEST
contract_rows = (((0,), (0,)), ((), ()))
contract_cols = (((1,), (1,)), ((), ()))


def split_up(shard, dim, peers):
    shape = shard.shape
    parts = shard.reshape(*shape[:dim], peers, shape[dim] // peers, *shape[dim + 1 :])
    return jnp.moveaxis(parts, dim, 0)


def sent_and_summed(shard, axis, dim):
    parts = split_up(shard, dim, lax.axis_size(axis))
    arrived = lax.all_to_all(parts, axis, split_axis=0, concat_axis=0, tiled=True)
    return arrived.astype(jnp.float32).sum(axis=0)


def in_one_piece(arrays, axis, dim, along):
    ends, at = ([], 0)
    for a in arrays[:-1]:
        at += a.shape[along]
        ends.append(at)
    both = jnp.concatenate(arrays, axis=along)
    return tuple(jnp.split(sent_and_summed(both, axis, dim), ends, axis=along))


def layer_stats(values, gain_vec, shift_vec):
    center = values - jnp.mean(values, -1, keepdims=True)
    factor = lax.rsqrt(jnp.mean(center * center, -1, keepdims=True) + norm_eps)
    normed = center * factor
    return (normed * gain_vec + shift_vec, normed, factor)


def layer_back(grad, normed, factor, gain_vec):
    scaled = grad * gain_vec
    return factor * (
        scaled
        - jnp.mean(scaled, -1, keepdims=True)
        - normed * jnp.mean(scaled * normed, -1, keepdims=True)
    )


def gelu_exact(values):
    return 0.5 * values * (1.0 + jax.scipy.special.erf(values * 0.7071067811865476))


def gelu_slope(values):
    return (
        0.5 * (1.0 + jax.scipy.special.erf(values * 0.7071067811865476))
        + values * jnp.exp(-0.5 * values * values) * 0.3989422804014327
    )


def rel_bias(rel_index, rel_table):
    seq_len = rel_index.shape[0]
    table_rows, heads = rel_table.shape
    blocks = rel_index.reshape(8, seq_len // 8, seq_len)

    def one_block(index_rows):
        onehot = (
            index_rows[:, :, None] == jnp.arange(table_rows, dtype=jnp.int32)[None, None, :]
        ).astype(jnp.float32)
        return jnp.einsum("qkr,rh->hqk", onehot, rel_table, precision=exact_prec)

    pieces = lax.map(one_block, blocks)
    return jnp.transpose(pieces, (1, 0, 2, 3)).reshape(heads, seq_len, seq_len)


def table_grad(rel_index, grad_rel, table_rows):
    heads, seq_len = (grad_rel.shape[0], grad_rel.shape[1])
    index_blocks = rel_index.reshape(8, seq_len // 8, seq_len)
    grad_blocks = jnp.moveaxis(grad_rel.reshape(heads, 8, seq_len // 8, seq_len), 1, 0)

    def add_block(total, paired):
        index_rows, grad_rows = paired
        onehot = (
            index_rows[:, :, None] == jnp.arange(table_rows, dtype=jnp.int32)[None, None, :]
        ).astype(jnp.float32)
        return (total + jnp.einsum("qkr,hqk->rh", onehot, grad_rows, precision=exact_prec), None)

    total, unused = lax.scan(
        add_block, jnp.zeros((table_rows, heads), jnp.float32), (index_blocks, grad_blocks)
    )
    return total


def adam_update(master, mean, square, grad, rate, decay):
    mean_new = beta_one * mean + (1.0 - beta_one) * grad
    square_new = beta_two * square + (1.0 - beta_two) * grad * grad
    fix_one = 1.0 - beta_one**STEP
    fix_two = 1.0 - beta_two**STEP
    direction = mean_new / fix_one / (jnp.sqrt(square_new / fix_two) + adam_eps)
    return (mean_new, square_new, master - rate * (direction + decay * master))


def shards(
    block_in,
    out_grad,
    mim_mask,
    rel_index,
    qkv_weight,
    proj_weight,
    up_weight,
    down_weight,
    vectors,
    up_bias,
    rel_table,
    qkv_master,
    qkv_mean,
    qkv_square,
    proj_master,
    proj_mean,
    proj_square,
    up_master,
    up_mean,
    up_square,
    down_master,
    down_mean,
    down_square,
    vector_mean,
    vector_square,
    bias_mean,
    bias_square,
    table_mean,
    table_square,
):
    images, seq_len, width = block_in.shape
    table_rows, heads = rel_table.shape
    head_dim = width // heads
    token_rows = images * seq_len
    factor_scale = head_dim ** (-0.5)
    local_ff = up_weight.shape[1]
    offset = lax.axis_index("narrow") * local_ff
    inputs = block_in.reshape(token_rows, width).astype(jnp.float32)
    first_norm, hat_one, factor_one = layer_stats(inputs, vectors[4], vectors[5])
    first_b = first_norm.astype(jnp.bfloat16)
    qkv_bias = jnp.concatenate([vectors[0], jnp.zeros_like(vectors[0]), vectors[1]])
    qkv_b = (jnp.dot(first_b, qkv_weight, preferred_element_type=jnp.float32) + qkv_bias).astype(
        jnp.bfloat16
    )
    parts = qkv_b.reshape(images, seq_len, 3, heads, head_dim)
    query, keys, values = (parts[:, :, 0], parts[:, :, 1], parts[:, :, 2])
    bias_all = rel_bias(rel_index, rel_table)
    key_keep = (jnp.arange(seq_len) < VALID)[None, None, None, :]

    def score_block():
        raw = (
            jnp.einsum("bqhd,bkhd->bhqk", query, keys, preferred_element_type=jnp.float32)
            * factor_scale
            + bias_all[None]
        )
        return jnp.where(key_keep, raw, -1e30)

    scores = score_block()
    log_total = jax.nn.logsumexp(scores, -1, keepdims=True)
    probs_b = jnp.exp(scores - log_total).astype(jnp.bfloat16)
    mixed = jnp.einsum("bhqk,bkhd->bqhd", probs_b, values, preferred_element_type=jnp.float32)
    heads_b = mixed.reshape(token_rows, width).astype(jnp.bfloat16)
    attn = jnp.dot(heads_b, proj_weight, preferred_element_type=jnp.float32) + vectors[2]
    middle = inputs + vectors[8] * attn
    second_norm, hat_two, factor_two = layer_stats(middle, vectors[6], vectors[7])
    second_b = second_norm.astype(jnp.bfloat16)
    gathered = lax.all_gather(second_b, "narrow", axis=0, tiled=True)
    local_bias = lax.dynamic_slice_in_dim(up_bias, offset, local_ff)
    hidden_pre = jnp.dot(gathered, up_weight, preferred_element_type=jnp.float32) + local_bias
    active_b = gelu_exact(hidden_pre).astype(jnp.bfloat16)
    block_rows = active_b
    branch = lax.psum_scatter(
        lax.dot_general(
            block_rows, down_weight, contract_cols, preferred_element_type=jnp.float32
        ).astype(jnp.bfloat16),
        "narrow",
        scatter_dimension=0,
        tiled=True,
    ).astype(jnp.float32)
    mlp_out = branch + vectors[3]
    block_out = (middle + vectors[9] * mlp_out).astype(jnp.bfloat16).reshape(images, seq_len, width)
    cotangent = out_grad.reshape(token_rows, width).astype(jnp.float32) * mim_mask.reshape(
        token_rows, 1
    ).astype(jnp.float32)
    grad_scale_two = jnp.sum(cotangent * mlp_out, 0)
    down_in_b = (vectors[9] * cotangent).astype(jnp.bfloat16)
    grad_down_bias = jnp.sum(down_in_b, 0, dtype=jnp.float32)
    down_all = lax.all_gather(down_in_b, "narrow", axis=0, tiled=True)
    active_grad = jnp.dot(down_all, down_weight, preferred_element_type=jnp.float32)
    grad_down = lax.dot_general(
        down_all, active_b, contract_rows, preferred_element_type=jnp.float32
    )
    pre_grad_b = (active_grad * gelu_slope(hidden_pre)).astype(jnp.bfloat16)
    grad_up = lax.dot_general(
        gathered, pre_grad_b, contract_rows, preferred_element_type=jnp.float32
    )
    local_bias_grad = jnp.sum(pre_grad_b, 0, dtype=jnp.float32)
    grad_bias = lax.dynamic_update_slice_in_dim(
        jnp.zeros(up_bias.shape, jnp.float32), local_bias_grad, offset, 0
    )
    block_rows = pre_grad_b
    grad_second = lax.psum_scatter(
        lax.dot_general(block_rows, up_weight, contract_cols, preferred_element_type=jnp.float32),
        "narrow",
        scatter_dimension=0,
        tiled=True,
    )
    grad_gain_two = jnp.sum(grad_second * hat_two, 0)
    grad_shift_two = jnp.sum(grad_second, 0)
    grad_middle = cotangent + layer_back(grad_second, hat_two, factor_two, vectors[6])
    grad_scale_one = jnp.sum(grad_middle * attn, 0)
    proj_in_b = (vectors[8] * grad_middle).astype(jnp.bfloat16)
    grad_proj_bias = jnp.sum(proj_in_b, 0, dtype=jnp.float32)
    grad_proj = lax.dot_general(
        heads_b, proj_in_b, contract_rows, preferred_element_type=jnp.float32
    )
    heads_grad_b = lax.dot_general(
        proj_in_b, proj_weight, contract_cols, preferred_element_type=jnp.float32
    ).astype(jnp.bfloat16)
    out_heads = heads_grad_b.reshape(images, seq_len, heads, head_dim)
    probs = jnp.exp(score_block() - log_total)
    probs_b = probs.astype(jnp.bfloat16)
    grad_values = jnp.einsum(
        "bhqk,bqhd->bkhd", probs_b, out_heads, preferred_element_type=jnp.float32
    )
    grad_probs = jnp.einsum(
        "bqhd,bkhd->bhqk", out_heads, values, preferred_element_type=jnp.float32
    )
    row_total = jnp.sum(grad_probs * probs, -1, keepdims=True)
    grad_scores_b = (probs * (grad_probs - row_total)).astype(jnp.bfloat16)
    grad_query = (
        jnp.einsum("bhqk,bkhd->bqhd", grad_scores_b, keys, preferred_element_type=jnp.float32)
        * factor_scale
    )
    grad_keys = (
        jnp.einsum("bhqk,bqhd->bkhd", grad_scores_b, query, preferred_element_type=jnp.float32)
        * factor_scale
    )
    grad_rel = jnp.sum(grad_scores_b, 0, dtype=jnp.float32)
    grad_table = table_grad(rel_index, grad_rel, table_rows)
    grad_qkv_b = (
        jnp.stack([grad_query, grad_keys, grad_values], 2)
        .reshape(token_rows, 3 * width)
        .astype(jnp.bfloat16)
    )
    column_sums = jnp.sum(grad_qkv_b, 0, dtype=jnp.float32)
    grad_qkv = lax.dot_general(
        first_b, grad_qkv_b, contract_rows, preferred_element_type=jnp.float32
    )
    grad_first = lax.dot_general(
        grad_qkv_b, qkv_weight, contract_cols, preferred_element_type=jnp.float32
    )
    grad_gain_one = jnp.sum(grad_first * hat_one, 0)
    grad_shift_one = jnp.sum(grad_first, 0)
    input_grad = (grad_middle + layer_back(grad_first, hat_one, factor_one, vectors[4])).reshape(
        images, seq_len, width
    )
    grad_vectors = jnp.stack(
        [
            column_sums[:width],
            column_sums[2 * width :],
            grad_proj_bias,
            grad_down_bias,
            grad_gain_one,
            grad_shift_one,
            grad_gain_two,
            grad_shift_two,
            grad_scale_one,
            grad_scale_two,
        ]
    )
    grad_vectors, grad_bias, grad_table = lax.psum(
        (grad_vectors, grad_bias, grad_table), ("wide", "narrow")
    )
    qkv_part, proj_part = (
        lax.psum_scatter(
            grad_qkv.astype(jnp.bfloat16), "narrow", scatter_dimension=1, tiled=True
        ).astype(jnp.float32),
        lax.psum_scatter(
            grad_proj.astype(jnp.bfloat16), "narrow", scatter_dimension=1, tiled=True
        ).astype(jnp.float32),
    )
    up_part, down_part = (grad_up, grad_down)
    qkv_shard, proj_shard, up_shard, down_shard = in_one_piece(
        (
            qkv_part.astype(jnp.bfloat16),
            proj_part.astype(jnp.bfloat16),
            up_part.astype(jnp.bfloat16),
            down_part.astype(jnp.bfloat16),
        ),
        "wide",
        0,
        1,
    )
    shard_squares = (
        jnp.sum(qkv_shard * qkv_shard)
        + jnp.sum(proj_shard * proj_shard)
        + jnp.sum(up_shard * up_shard)
        + jnp.sum(down_shard * down_shard)
    )
    large_squares = lax.psum(shard_squares, ("wide", "narrow"))
    small_squares = (
        jnp.sum(grad_vectors * grad_vectors)
        + jnp.sum(grad_bias * grad_bias)
        + jnp.sum(grad_table * grad_table)
    )
    grad_norm = jnp.sqrt(large_squares + small_squares)
    clip = jnp.minimum(1.0, max_norm / (grad_norm + clip_eps))
    results = [block_out, input_grad, grad_norm]
    for master, mean, square, grad in (
        (qkv_master, qkv_mean, qkv_square, qkv_shard),
        (proj_master, proj_mean, proj_square, proj_shard),
        (up_master, up_mean, up_square, up_shard),
        (down_master, down_mean, down_square, down_shard),
    ):
        mean_new, square_new, master_new = adam_update(
            master, mean, square, clip * grad, rate_matrix, weight_decay
        )
        results += [mean_new, square_new, master_new, master_new.astype(jnp.bfloat16)]
    for master, mean, square, grad in (
        (vectors, vector_mean, vector_square, grad_vectors),
        (up_bias, bias_mean, bias_square, grad_bias),
        (rel_table, table_mean, table_square, grad_table),
    ):
        mean_new, square_new, master_new = adam_update(
            master, mean, square, clip * grad, rate_small, 0.0
        )
        results += [mean_new, square_new, master_new]
    return tuple(results)


def solution(mesh):
    in_specs = (
        P(("wide", "narrow"), None, None),
        P(("wide", "narrow"), None, None),
        P(("wide", "narrow"), None),
        P(),
        P(),
        P(),
        P(None, "narrow"),
        P(None, "narrow"),
        P(),
        P(),
        P(),
        P("wide", "narrow"),
        P("wide", "narrow"),
        P("wide", "narrow"),
        P("wide", "narrow"),
        P("wide", "narrow"),
        P("wide", "narrow"),
        P("wide", "narrow"),
        P("wide", "narrow"),
        P("wide", "narrow"),
        P("wide", "narrow"),
        P("wide", "narrow"),
        P("wide", "narrow"),
        P(),
        P(),
        P(),
        P(),
        P(),
        P(),
    )
    out_specs = (
        P(("wide", "narrow"), None, None),
        P(("wide", "narrow"), None, None),
        P(),
        P("wide", "narrow"),
        P("wide", "narrow"),
        P("wide", "narrow"),
        P("wide", "narrow"),
        P("wide", "narrow"),
        P("wide", "narrow"),
        P("wide", "narrow"),
        P("wide", "narrow"),
        P("wide", "narrow"),
        P("wide", "narrow"),
        P("wide", "narrow"),
        P("wide", "narrow"),
        P("wide", "narrow"),
        P("wide", "narrow"),
        P("wide", "narrow"),
        P("wide", "narrow"),
        P(),
        P(),
        P(),
        P(),
        P(),
        P(),
        P(),
        P(),
        P(),
    )
    return jax.shard_map(shards, mesh=mesh, in_specs=in_specs, out_specs=out_specs, check_vma=False)
```

profile of v0, /device:TPU:0, one launch (start us, length us, event | category | flops | bytes accessed | tf_op | source)
XLA Modules:
  0.0 806.3 jit_solution(16619423688516278176)
XLA Ops:
  17.9 79.3 %while.21 = (s32[]{:T(128)}, f32[8,12,25,200]{3,1,2,0:T(8,128)}, s32[8,25,200]{2,1,0:T(8,128)}, f32[732,12]{0,1:T(8,128)}, s32[]{:T(128)}) while((s32[]{:T(128)}, f32[8,12,25,200]{3,1,2,0:T(8,128)}, s32[8,25,200]{2,1,0:T(8,128)}, f32[732,12]{0,1:T(8,128)}, s32[]{:T(128)}) %tuple.94), condition=%wide.region_3.4_spmd, body=%wide.region_2.3_spmd.sunk | while | flops 530700000 | bytes 518829 | solution.py:81
  18.6 9.1 %fusion.86 = f32[8,12,25,200]{3,1,2,0:T(8,128)} fusion(f32[8,12,25,200]{3,1,2,0:T(8,128)} %get-tuple-element.246, s32[]{:T(128)S(6)} %copy.134, s32[25,200]{1,0:T(8,128)S(1)} %dynamic-slice_bitcast_fusion.4, f32[732,12]{0,1:T(8,128)} %get-tuple-element.253), kind=kOutput, calls=%fused_computation.4.clone.1 | convolution fusion | flops 530700000 | bytes 478756 | tf_op jit(solution)/shard_map/while/body/eval_jaxpr/qkr,rh->hqk/dot_general | solution.py:79
  28.5 9.1 %fusion.86 = f32[8,12,25,200]{3,1,2,0:T(8,128)} fusion(f32[8,12,25,200]{3,1,2,0:T(8,128)} %get-tuple-element.246, s32[]{:T(128)S(6)} %copy.134, s32[25,200]{1,0:T(8,128)S(1)} %dynamic-slice_bitcast_fusion.4, f32[732,12]{0,1:T(8,128)} %get-tuple-element.253), kind=kOutput, calls=%fused_computation.4.clone.1 | convolution fusion | flops 530700000 | bytes 478756 | tf_op jit(solution)/shard_map/while/body/eval_jaxpr/qkr,rh->hqk/dot_general | solution.py:79
  38.5 9.2 %fusion.86 = f32[8,12,25,200]{3,1,2,0:T(8,128)} fusion(f32[8,12,25,200]{3,1,2,0:T(8,128)} %get-tuple-element.246, s32[]{:T(128)S(6)} %copy.134, s32[25,200]{1,0:T(8,128)S(1)} %dynamic-slice_bitcast_fusion.4, f32[732,12]{0,1:T(8,128)} %get-tuple-element.253), kind=kOutput, calls=%fused_computation.4.clone.1 | convolution fusion | flops 530700000 | bytes 478756 | tf_op jit(solution)/shard_map/while/body/eval_jaxpr/qkr,rh->hqk/dot_general | solution.py:79
  48.4 9.1 %fusion.86 = f32[8,12,25,200]{3,1,2,0:T(8,128)} fusion(f32[8,12,25,200]{3,1,2,0:T(8,128)} %get-tuple-element.246, s32[]{:T(128)S(6)} %copy.134, s32[25,200]{1,0:T(8,128)S(1)} %dynamic-slice_bitcast_fusion.4, f32[732,12]{0,1:T(8,128)} %get-tuple-element.253), kind=kOutput, calls=%fused_computation.4.clone.1 | convolution fusion | flops 530700000 | bytes 478756 | tf_op jit(solution)/shard_map/while/body/eval_jaxpr/qkr,rh->hqk/dot_general | solution.py:79
  58.3 9.1 %fusion.86 = f32[8,12,25,200]{3,1,2,0:T(8,128)} fusion(f32[8,12,25,200]{3,1,2,0:T(8,128)} %get-tuple-element.246, s32[]{:T(128)S(6)} %copy.134, s32[25,200]{1,0:T(8,128)S(1)} %dynamic-slice_bitcast_fusion.4, f32[732,12]{0,1:T(8,128)} %get-tuple-element.253), kind=kOutput, calls=%fused_computation.4.clone.1 | convolution fusion | flops 530700000 | bytes 478756 | tf_op jit(solution)/shard_map/while/body/eval_jaxpr/qkr,rh->hqk/dot_general | solution.py:79
  68.2 9.2 %fusion.86 = f32[8,12,25,200]{3,1,2,0:T(8,128)} fusion(f32[8,12,25,200]{3,1,2,0:T(8,128)} %get-tuple-element.246, s32[]{:T(128)S(6)} %copy.134, s32[25,200]{1,0:T(8,128)S(1)} %dynamic-slice_bitcast_fusion.4, f32[732,12]{0,1:T(8,128)} %get-tuple-element.253), kind=kOutput, calls=%fused_computation.4.clone.1 | convolution fusion | flops 530700000 | bytes 478756 | tf_op jit(solution)/shard_map/while/body/eval_jaxpr/qkr,rh->hqk/dot_general | solution.py:79
  78.1 9.2 %fusion.86 = f32[8,12,25,200]{3,1,2,0:T(8,128)} fusion(f32[8,12,25,200]{3,1,2,0:T(8,128)} %get-tuple-element.246, s32[]{:T(128)S(6)} %copy.134, s32[25,200]{1,0:T(8,128)S(1)} %dynamic-slice_bitcast_fusion.4, f32[732,12]{0,1:T(8,128)} %get-tuple-element.253), kind=kOutput, calls=%fused_computation.4.clone.1 | convolution fusion | flops 530700000 | bytes 478756 | tf_op jit(solution)/shard_map/while/body/eval_jaxpr/qkr,rh->hqk/dot_general | solution.py:79
  88.0 9.2 %fusion.86 = f32[8,12,25,200]{3,1,2,0:T(8,128)} fusion(f32[8,12,25,200]{3,1,2,0:T(8,128)} %get-tuple-element.246, s32[]{:T(128)S(6)} %copy.134, s32[25,200]{1,0:T(8,128)S(1)} %dynamic-slice_bitcast_fusion.4, f32[732,12]{0,1:T(8,128)} %get-tuple-element.253), kind=kOutput, calls=%fused_computation.4.clone.1 | convolution fusion | flops 530700000 | bytes 478756 | tf_op jit(solution)/shard_map/while/body/eval_jaxpr/qkr,rh->hqk/dot_general | solution.py:79
  97.2 4.7 copy.102
  102.6 8.1 %add_convert_fusion = bf16[1000,2304]{1,0:T(8,128)(2,1)} fusion(bf16[768,2304]{1,0:T(8,128)(2,1)S(1)} %copy-done, f32[2304]{0:T(1024)S(1)} %pad_maximum_fusion.1, f32[768]{0:T(1024)} %get-tuple-element.109, f32[768]{0:T(1024)S(1)} %copy-done.26, f32[1000]{0:T(1024)} %rsqrt.21, f32[1000]{0:T(1024)S(1)} %copy-done.28, bf16[1000,768]{1,0:T(8,128)(2,1)} %bitcast.124), kind=kOutput, calls=%fused_computation.34 | convolution fusion | flops 3548160000 | bytes 9706304 | tf_op jit(solution)/shard_map/dot_general | solution.py:154
  110.7 14.9 %reshape.239 = bf16[5,200,3,12,64]{4,3,2,1,0:T(8,128)(2,1)} reshape(bf16[1000,2304]{1,0:T(8,128)(2,1)} %add_convert_fusion) | data formatting | bytes 9216000 | tf_op jit(solution)/shard_map/reshape | solution.py:157
  125.6 8.4 %fusion.50 = (bf16[5,200,1,12,64]{4,3,2,1,0:T(8,128)(2,1)}, bf16[5,200,1,12,64]{4,3,2,1,0:T(8,128)(2,1)}, bf16[5,200,1,12,64]{4,3,2,1,0:T(8,128)(2,1)}) fusion(bf16[5,200,3,12,64]{4,3,2,1,0:T(8,128)(2,1)} %reshape.239), kind=kLoop, calls=%fused_computation.151 | loop fusion | bytes 9216000 | tf_op jit(solution)/shard_map/slice | solution.py:158
  134.0 6.0 copy.125
  140.0 6.0 copy.124
  146.0 6.2 copy.126
  152.2 6.2 fusion.52
  158.5 2.9 exponential_reduce_fusion
  165.5 3.1 copy.104
  168.6 6.0 convert_element_type.161
  174.6 6.4 multiply_add_fusion.2
  190.7 2.9 multiply_convert_fusion.4
  195.1 41.3 %all-gather.3.cloned.1.call-done = bf16[4000,768]{1,0:T(8,128)(2,1)} async-done(((bf16[1000,768]{1,0:T(8,128)(2,1)}), bf16[4000,768]{1,0:T(8,128)(2,1)}) %all-gather.3.cloned.1.call-update) | async-done | bytes 6144016 | tf_op jit(solution)/shard_map/all_gather | solution.py:179
  236.4 12.7 %multiply_convert_fusion.1 = (bf16[4000,768]{1,0:T(8,128)(2,1)}, f32[4000,768]{1,0:T(8,128)}) fusion(f32[768]{0:T(1024)} %dynamic_slice.14, bf16[4000,768]{1,0:T(8,128)(2,1)} %all-gather.3.cloned.1.call-done, bf16[768,768]{1,0:T(8,128)(2,1)} %param.39), kind=kOutput, calls=%fused_computation.26 | convolution fusion | flops 4737024000 | bytes 25758720 | tf_op jit(solution)/shard_map/dot_general | solution.py:181
  249.0 34.4 %all-gather.5.cloned.1.call-done = bf16[4000,768]{1,0:T(8,128)(2,1)} async-done(((bf16[1000,768]{1,0:T(8,128)(2,1)}), bf16[4000,768]{1,0:T(8,128)(2,1)}) %all-gather.5.cloned.1.call-update) | async-done | bytes 6144016 | tf_op jit(solution)/shard_map/all_gather | solution.py:200
  283.5 12.4 %convert_reduce_fusion.1 = (f32[768]{0:T(1024)}, bf16[4000,768]{1,0:T(8,128)(2,1)S(1)}) fusion(f32[4000,768]{1,0:T(8,128)} %get-tuple-element.182, f32[768]{0:T(1024)} %dynamic_slice.14, bf16[4000,768]{1,0:T(8,128)(2,1)} %all-gather.5.cloned.1.call-done, bf16[768,768]{1,0:T(8,128)(2,1)} %param.40), kind=kOutput, calls=%fused_computation.23 | convolution fusion | flops 4758526976 | bytes 25761792 | tf_op jit(solution)/shard_map/dot_general | solution.py:201
  298.6 7.9 fusion.54
  306.8 12.6 %convolution_convert_fusion = bf16[4000,768]{1,0:T(8,128)(2,1)} fusion(bf16[4000,768]{1,0:T(8,128)(2,1)} %get-tuple-element.181, bf16[768,768]{1,0:T(8,128)(2,1)} %param.40), kind=kOutput, calls=%fused_computation.36 | convolution fusion | flops 4721664000 | bytes 13467648 | tf_op jit(solution)/shard_map/dot_general | solution.py:185
  319.4 3.8 add_convert_fusion.1
  323.2 81.1 %reduce-scatter.7.cloned.1.call-done = f32[1000,768]{1,0:T(8,128)} async-done(((f32[4000,768]{1,0:T(8,128)}), f32[1000,768]{1,0:T(8,128)}) %reduce-scatter.7.cloned.1.call-update) | async-done | bytes 3072016 | tf_op jit(solution)/shard_map/reduce_scatter | solution.py:214
  404.3 4.2 multiply_reduce_fusion.3
  409.2 55.5 %reduce-scatter.5.cloned.1.call-done = bf16[1000,768]{1,0:T(8,128)(2,1)} async-done(((bf16[4000,768]{1,0:T(8,128)(2,1)}), bf16[1000,768]{1,0:T(8,128)(2,1)}) %reduce-scatter.5.cloned.1.call-update) | async-done | bytes 1536016 | tf_op jit(solution)/shard_map/reduce_scatter | solution.py:184
  464.6 8.4 %multiply_reduce_fusion.2 = (f32[768]{0:T(1024)}, f32[1000,768]{1,0:T(8,128)S(1)}, bf16[1000,768]{1,0:T(8,128)(2,1)}, f32[768]{0:T(1024)}) fusion(f32[1000,768]{1,0:T(8,128)} %get-tuple-element.180, f32[768]{0:T(1024)} %get-tuple-element.106, f32[1000]{0:T(1024)} %get-tuple-element.188, f32[1000,768]{1,0:T(8,128)} %get-tuple-element.179, ...), kind=kLoop, calls=%fused_computation.43 | loop fusion | flops 15358464 | bytes 16934432 | tf_op jit(solution)/shard_map/reduce_sum | solution.py:223
  479.4 4.3 convolution_convert_fusion.2
  484.2 5.8 reshape.240
  490.0 6.1 copy.106
  496.0 13.1 %multiply_reduce_fusion = (f32[5,12,200]{2,1,0:T(8,128)S(1)}, f32[5,12,200,200]{2,3,1,0:T(8,128)}) fusion(f32[5,12,200,200]{2,3,1,0:T(8,128)} %copy-done.1, f32[5,12,200]{2,1,0:T(8,128)} %copy-done.9, bf16[5,200,12,64]{1,3,2,0:T(8,128)(2,1)} %copy.106, bf16[5,200,1,12,64]{1,4,3,0,2:T(8,128)(2,1)} %copy.124), kind=kOutput, calls=%fused_computation.25 | convolution fusion | flops 314388000 | bytes 22368000 | tf_op jit(solution)/shard_map/bqhd,bkhd->bhqk/dot_general | solution.py:238
  509.1 12.1 %convert_reduce_fusion = (f32[12,200,200]{1,2,0:T(8,128)}, bf16[5,12,200,200]{2,3,1,0:T(8,128)(2,1)S(1)}) fusion(f32[5,12,200,200]{2,3,1,0:T(8,128)} %get-tuple-element.184, f32[5,12,200]{2,1,0:T(8,128)S(1)} %get-tuple-element.183, f32[5,12,200,200]{2,3,1,0:T(8,128)} %copy-done.1, f32[5,12,200]{2,1,0:T(8,128)S(1)} %copy-done.10), kind=kLoop, calls=%fused_computation.22 | loop fusion | flops 13920000 | bytes 26016000 | tf_op jit(solution)/shard_map/reduce_sum | solution.py:251
  521.2 5.1 multiply_bitcast_fusion
  529.0 5.1 convolution_bitcast_fusion
  534.1 6.6 convert_reduce_fusion.2
  540.7 11.3 %copy.111 = bf16[5,200,3,12,64]{1,0,4,3,2:T(8,128)(2,1)} copy(bf16[5,200,3,12,64]{1,4,3,0,2:T(8,128)(2,1)} %get-tuple-element.165) | data formatting | bytes 9216000 | tf_op jit(solution)/shard_map/convert_element_type | solution.py:256
  552.0 13.8 %convert_element_type.177 = bf16[1000,2304]{0,1:T(8,128)(2,1)} reshape(bf16[5,200,3,12,64]{1,0,4,3,2:T(8,128)(2,1)} %copy.111) | data formatting | bytes 9216000 | tf_op jit(solution)/shard_map/convert_element_type | solution.py:256
  565.8 8.4 %convolution_convert_fusion.1 = bf16[768,2304]{0,1:T(8,128)(2,1)} fusion(bf16[1000,768]{1,0:T(8,128)(2,1)} %bitcast.131, bf16[1000,2304]{0,1:T(8,128)(2,1)} %convert_element_type.177), kind=kOutput, calls=%fused_computation.37 | convolution fusion | flops 3540713472 | bytes 9682944 | tf_op jit(solution)/shard_map/dot_general | solution.py:259
  574.2 9.8 %convolution_convert_fusion.3 = bf16[768,768]{0,1:T(8,128)(2,1)} fusion(bf16[4000,768]{1,0:T(8,128)(2,1)} %all-gather.5.cloned.1.call-done, bf16[4000,768]{1,0:T(8,128)(2,1)} %get-tuple-element.181), kind=kOutput, calls=%fused_computation.79 | convolution fusion | flops 4719181824 | bytes 13467648 | tf_op jit(solution)/shard_map/dot_general | solution.py:202
  584.0 10.0 %convolution_convert_fusion.4 = bf16[768,768]{0,1:T(8,128)(2,1)} fusion(bf16[4000,768]{1,0:T(8,128)(2,1)} %all-gather.3.cloned.1.call-done, bf16[4000,768]{1,0:T(8,128)(2,1)} %copy-done.35), kind=kOutput, calls=%fused_computation.80 | convolution fusion | flops 4719181824 | bytes 13467648 | tf_op jit(solution)/shard_map/dot_general | solution.py:206
  594.1 20.7 %reduce-scatter.9.cloned.1.call-done = bf16[768,576]{0,1:T(8,128)(2,1)} async-done(((bf16[768,2304]{0,1:T(8,128)(2,1)}), bf16[768,576]{0,1:T(8,128)(2,1)}) %reduce-scatter.9.cloned.1.call-update) | async-done | bytes 884752 | tf_op jit(solution)/shard_map/reduce_scatter | solution.py:288
  614.7 3.5 pad_maximum_fusion
  618.2 5.8 copy.112
  624.0 5.9 all-to-all-start
  639.6 3.2 copy.113
  646.9 3.6 reshape.234
  650.4 10.1 %multiply_reduce_fusion.4 = (f32[768]{0:T(1024)S(1)}, f32[1000]{0:T(1024)}, f32[1000]{0:T(1024)}, f32[768]{0:T(1024)S(1)}, f32[1000,768]{1,0:T(8,128)}) fusion(f32[1000]{0:T(1024)} %rsqrt.21, f32[1000]{0:T(1024)} %div.123, bf16[5,200,768]{2,1,0:T(8,128)(2,1)} %param.33, f32[768]{0:T(1024)S(1)} %copy-done.27, bf16[1000,2304]{0,1:T(8,128)(2,1)} %convert_element_type.177, ...), kind=kOutput, calls=%fused_computation.45 | convolution fusion | flops 3548924416 | bytes 14316160 | tf_op jit(solution)/shard_map/dot_general | solution.py:262
  665.9 5.9 multiply_add_fusion
  671.8 60.1 %while.22 = (s32[]{:T(128)}, f32[732,12]{0,1:T(8,128)}, s32[8,25,200]{2,1,0:T(8,128)}, f32[8,12,25,200]{3,2,0,1:T(8,128)}, s32[]{:T(128)}, /*index=5*/s32[]{:T(128)}) while((s32[]{:T(128)}, f32[732,12]{0,1:T(8,128)}, s32[8,25,200]{2,1,0:T(8,128)}, f32[8,12,25,200]{3,2,0,1:T(8,128)}, s32[]{:T(128)}, /*index=5*/s32[]{:T(128)}) %tuple.113), condition=%wide.region_39.40_spmd.clone, body=%wide.region_38.39_spmd.clone.sunk | while | flops 530717568 | bytes 850367 | solution.py:97
  673.5 5.0 fusion.87
  680.3 5.8 fusion.87
  687.9 5.8 fusion.87
  695.5 5.8 fusion.87
  703.1 5.8 fusion.87
  710.7 5.8 fusion.87
  718.2 5.8 fusion.87
  725.8 5.8 fusion.87
  739.2 41.4 %all-reduce.2 = (f32[]{:T(128)}, f32[10,768]{1,0:T(8,128)}, f32[3072]{0:T(1024)}, f32[732,12]{0,1:T(8,128)}) all-reduce(f32[]{:T(128)S(6)} %add.302, f32[10,768]{1,0:T(8,128)} %stack.59, f32[3072]{0:T(1024)S(1)} %dynamic_update_slice.7, f32[732,12]{0,1:T(8,128)} %get-tuple-element.73), channel_id=1, replica_groups=mesh['wide'=8,'narrow'=4] {'wide','narrow'}, use_global_device_ids=true, to_apply=%region_22.23 | all-reduce | flops 19537 | bytes 156296 | tf_op jit(solution)/shard_map/psum | solution.py:313
  (175 shorter events, 98.1 us)
Async XLA Ops:
  7.2 95.4 %copy-start = (bf16[768,2304]{1,0:T(8,128)(2,1)S(1)}, bf16[768,2304]{1,0:T(8,128)(2,1)}, u32[]{:S(2)}) copy-start(bf16[768,2304]{1,0:T(8,128)(2,1)} %param.37) | copy-start | bytes 10616836
  7.2 229.1 %all-gather.3.cloned.1.call-start = ((), (), s32[]{:S(2)}) async-start(), calls=%async_computation.5 | async-start | bytes 7680000 | tf_op jit(solution)/shard_map/all_gather | solution.py:179
  13.7 4.2 copy-start.20
  97.2 5.4 copy-start.26
  97.2 5.4 copy-start.28
  146.0 6.2 copy-start.33
  158.5 4.8 copy-start.1
  158.5 4.8 copy-start.5
  163.3 2.2 copy-start.9
  168.6 6.0 copy-start.29
  168.6 6.0 copy-start.32
  183.1 3.1 copy-start.2
  183.1 3.1 copy-start.22
  183.1 3.1 copy-start.31
  185.6 0.6 copy-start.24
  186.2 4.4 copy-start.21
  188.0 95.5 %all-gather.5.cloned.1.call-start = ((), (), s32[]{:S(2)}) async-start(), calls=%async_computation.7 | async-start | bytes 7680000 | tf_op jit(solution)/shard_map/all_gather | solution.py:200
  193.6 210.7 %reduce-scatter.7.cloned.1.call-start = ((), (), s32[]{:S(2)}) async-start(), calls=%async_computation.8 | async-start | bytes 15360000 | tf_op jit(solution)/shard_map/reduce_scatter | solution.py:214
  283.5 15.1 %copy-start.34 = (bf16[768,768]{1,0:T(8,128)(2,1)S(1)}, bf16[768,768]{1,0:T(8,128)(2,1)}, u32[]{:S(2)}) copy-start(bf16[768,768]{1,0:T(8,128)(2,1)} %param.39) | copy-start | bytes 3538948
  295.9 2.7 copy-start.35
  306.5 158.1 %reduce-scatter.5.cloned.1.call-start = ((), (), s32[]{:S(2)}) async-start(), calls=%async_computation.6 | async-start | bytes 7680000 | tf_op jit(solution)/shard_map/reduce_scatter | solution.py:184
  319.4 274.7 %reduce-scatter.11.cloned.1.call-start = ((), (), s32[]{:S(2)}) async-start(), calls=%async_computation.10 | async-start | bytes 1474560 | tf_op jit(solution)/shard_map/reduce_scatter | solution.py:291
  323.2 141.5 %copy-start.23 = (f32[768]{0:T(1024)S(1)}, f32[768]{0:T(1024)}, u32[]{:S(2)}) copy-start(f32[768]{0:T(1024)} %get-tuple-element.105) | copy-start | bytes 9220
  323.2 141.5 %copy-start.25 = (f32[1000]{0:T(1024)S(1)}, f32[1000]{0:T(1024)}, u32[]{:S(2)}) copy-start(f32[1000]{0:T(1024)} %copy-done.24) | copy-start | bytes 12004
  464.6 10.0 %copy-start.30 = (f32[768]{0:T(1024)S(1)}, f32[768]{0:T(1024)}, u32[]{:S(2)}) copy-start(f32[768]{0:T(1024)} %get-tuple-element.111) | copy-start | bytes 9220
  473.0 1.6 copy-start.3
  473.0 3.9 copy-start.11
  475.7 1.2 copy-start.12
  483.7 131.0 %reduce-scatter.9.cloned.1.call-start = ((), (), s32[]{:S(2)}) async-start(), calls=%async_computation.9 | async-start | bytes 4423680 | tf_op jit(solution)/shard_map/reduce_scatter | solution.py:288
  496.0 13.1 %copy-start.10 = (f32[5,12,200]{2,1,0:T(8,128)S(1)}, f32[5,12,200]{2,1,0:T(8,128)}, u32[]{:S(2)}) copy-start(f32[5,12,200]{2,1,0:T(8,128)} %copy-done.9) | copy-start | bytes 144004
  509.1 19.9 %slice-start = ((s8[12288000]{0:T(1024)(128)(4,1)}), s8[4194304]{0:T(1024)(128)(4,1)S(1)}, s32[]{:S(2)}) async-start(s8[12288000]{0:T(1024)(128)(4,1)} %bitcast.122), calls=%async_computation.11 | async-start | bytes 8388608
  509.1 19.9 %slice-start.1 = ((s8[12288000]{0:T(1024)(128)(4,1)}), s8[4194304]{0:T(1024)(128)(4,1)S(1)}, s32[]{:S(2)}) async-start(s8[12288000]{0:T(1024)(128)(4,1)} %bitcast.122), calls=%async_computation.12 | async-start | bytes 8388608
  521.2 5.1 copy-start.4
  521.2 7.8 slice-start.2
  529.0 5.1 copy-start.8
  624.0 5.9 copy-start.19
  624.0 107.8 %all-to-all-start = ((bf16[8,96,2304]{2,1,0:T(8,128)(2,1)}), bf16[8,96,2304]{2,1,0:T(8,128)(2,1)}, u32[]{:S(2)}, u32[]{:S(2)}) async-start(bf16[8,96,2304]{2,1,0:T(8,128)(2,1)} %bitcast.126), calls=%async_computation.4 | async-start | bytes 7077888 | tf_op jit(solution)/shard_map/all_to_all | solution.py:30
  642.8 7.6 copy-start.27
  734.4 1.5 copy-start.6
  787.4 8.9 %copy-start.7 = (f32[96,2304]{1,0:T(8,128)S(1)}, f32[96,2304]{1,0:T(8,128)}, u32[]{:S(2)}) copy-start(f32[96,2304]{1,0:T(8,128)} %copy-done.6) | copy-start | bytes 2654212
  787.4 8.9 %copy-start.13 = (f32[96,768]{1,0:T(8,128)S(1)}, f32[96,768]{1,0:T(8,128)}, u32[]{:S(2)}) copy-start(f32[96,768]{1,0:T(8,128)} %param.53) | copy-start | bytes 884740
  787.4 8.9 %copy-start.14 = (f32[96,768]{1,0:T(8,128)S(1)}, f32[96,768]{1,0:T(8,128)}, u32[]{:S(2)}) copy-start(f32[96,768]{1,0:T(8,128)} %param.55) | copy-start | bytes 884740
  787.5 8.9 %copy-start.15 = (f32[96,768]{1,0:T(8,128)S(1)}, f32[96,768]{1,0:T(8,128)}, u32[]{:S(2)}) copy-start(f32[96,768]{1,0:T(8,128)} %param.54) | copy-start | bytes 884740
  787.5 8.9 %copy-start.16 = (f32[96,768]{1,0:T(8,128)S(1)}, f32[96,768]{1,0:T(8,128)}, u32[]{:S(2)}) copy-start(f32[96,768]{1,0:T(8,128)} %param.50) | copy-start | bytes 884740
  787.5 8.9 %copy-start.17 = (f32[96,768]{1,0:T(8,128)S(1)}, f32[96,768]{1,0:T(8,128)}, u32[]{:S(2)}) copy-start(f32[96,768]{1,0:T(8,128)} %param.52) | copy-start | bytes 884740
  787.5 8.9 %copy-start.18 = (f32[96,768]{1,0:T(8,128)S(1)}, f32[96,768]{1,0:T(8,128)}, u32[]{:S(2)}) copy-start(f32[96,768]{1,0:T(8,128)} %param.51) | copy-start | bytes 884740
Sparse Core Ops, SparseCore 0:
  188.1 48.2 all-gather.2
  237.9 45.5 all-gather.4
  306.6 97.6 reduce-scatter.6
  406.7 57.8 reduce-scatter.4
  483.8 25.5 reduce-scatter.10
  574.3 40.3 reduce-scatter.8
where the time goes:
time: 818 us; the launch traced here: 806 us
  matrix products  258 us (32%)
  waiting for transfers between devices  233 us (28%)
  local copies, waits for them, and re-layouts  157 us (19%)
  other arithmetic  88.3 us (11%)
  blocking collectives  41.4 us (5%)
  between operations  21.4 us (3%)
    reduce_scatter x1, waiting for transfers between devices, shards(): lax.psum_scatter(lax.dot_general(block_rows, up_weight, contract_cols, pr...  81.1 us
    dot_general x8, matrix products, one_block(): return jnp.einsum('qkr,rh->hqk', onehot, rel_table, precision=exact_prec)  73.2 us
    reduce_scatter x1, waiting for transfers between devices, shards(): lax.psum_scatter(lax.dot_general(block_rows, down_weight, contract_cols,...  55.5 us
    dot_general x8, matrix products, add_block(): jnp.einsum('qkr,hqk->rh', onehot, grad_rows, precision=exact_prec)  45.6 us
    psum x1, blocking collectives, shards(): large_squares = lax.psum(shard_squares, ('wide', 'narrow'))  41.4 us
    all_gather x1, waiting for transfers between devices, shards(): gathered = lax.all_gather(second_b, 'narrow', axis=0, tiled=True)  41.3 us
    all_gather x1, waiting for transfers between devices, shards(): down_all = lax.all_gather(down_in_b, 'narrow', axis=0, tiled=True)  34.4 us
    unnamed x81, local copies, waits for them, and re-layouts  26.3 us
  transfers between devices with their start and end apart: 7, of which 5 were waited for; matrix products, arithmetic and copies ran while one was open for 31% of the time, Pallas kernels for 0%

commit v1 on v0

--- a/solution.py
+++ b/solution.py
@@ -310,7 +310,7 @@
         + jnp.sum(up_shard * up_shard)
         + jnp.sum(down_shard * down_shard)
     )
-    large_squares = lax.psum(shard_squares, ("wide", "narrow"))
+    large_squares = jax.lax.all_gather(shard_squares, axis_name=("wide", "narrow")).sum(axis=0)
     small_squares = (
         jnp.sum(grad_vectors * grad_vectors)
         + jnp.sum(grad_bias * grad_bias)

time: 818 us -> 897 us (1.097)
  waiting for transfers between devices: 233 us -> 351 us
  blocking collectives: 41.4 us -> 0 us
    unnamed x6 -> x8, waiting for transfers between devices: 0.1 us -> 119 us
    psum x1 -> x0, blocking collectives: 41.4 us -> none  [shards(): large_squares = lax.psum(shard_squares, ('wide', 'narrow'))]
    unnamed x81 -> x89, local copies, waits for them, and re-layouts: 26.3 us -> 27.1 us
  transfers between devices with their start and end apart: 7 -> 8, of which waited for: 5 -> 6; matrix products, arithmetic and copies ran while one was open for 31% -> 29% of each run, Pallas kernels for 0% -> 0%
where the time goes in v1:
time: 897 us; the launch traced here: 885 us
  waiting for transfers between devices  351 us (39%)
  matrix products  259 us (29%)
  local copies, waits for them, and re-layouts  156 us (17%)
  other arithmetic  90.7 us (10%)
  between operations  21.2 us (2%)
    unnamed x8, waiting for transfers between devices  119 us
    reduce_scatter x1, waiting for transfers between devices, shards(): lax.psum_scatter(lax.dot_general(block_rows, up_weight, contract_cols, pr...  80.8 us
    dot_general x8, matrix products, one_block(): return jnp.einsum('qkr,rh->hqk', onehot, rel_table, precision=exact_prec)  73.2 us
    reduce_scatter x1, waiting for transfers between devices, shards(): lax.psum_scatter(lax.dot_general(block_rows, down_weight, contract_cols,...  55.5 us
    dot_general x8, matrix products, add_block(): jnp.einsum('qkr,hqk->rh', onehot, grad_rows, precision=exact_prec)  45.6 us
    all_gather x1, waiting for transfers between devices, shards(): gathered = lax.all_gather(second_b, 'narrow', axis=0, tiled=True)  41.3 us
    all_gather x1, waiting for transfers between devices, shards(): down_all = lax.all_gather(down_in_b, 'narrow', axis=0, tiled=True)  34.4 us
    unnamed x89, local copies, waits for them, and re-layouts  27.1 us
  transfers between devices with their start and end apart: 8, of which 6 were waited for; matrix products, arithmetic and copies ran while one was open for 29% of the time, Pallas kernels for 0%

profile of v1, /device:TPU:0, one launch (start us, length us, event | category | flops | bytes accessed | tf_op | source)
XLA Modules:
  0.0 884.6 jit_solution(10924581168113825059)
XLA Ops:
  17.9 79.3 %while.21 = (s32[]{:T(128)}, f32[8,12,25,200]{3,1,2,0:T(8,128)}, s32[8,25,200]{2,1,0:T(8,128)}, f32[732,12]{0,1:T(8,128)}, s32[]{:T(128)}) while((s32[]{:T(128)}, f32[8,12,25,200]{3,1,2,0:T(8,128)}, s32[8,25,200]{2,1,0:T(8,128)}, f32[732,12]{0,1:T(8,128)}, s32[]{:T(128)}) %tuple.94), condition=%wide.region_3.4_spmd, body=%wide.region_2.3_spmd.sunk | while | flops 530700000 | bytes 518829 | solution.py:81
  18.6 9.1 %fusion.86 = f32[8,12,25,200]{3,1,2,0:T(8,128)} fusion(f32[8,12,25,200]{3,1,2,0:T(8,128)} %get-tuple-element.246, s32[]{:T(128)S(6)} %copy.134, s32[25,200]{1,0:T(8,128)S(1)} %dynamic-slice_bitcast_fusion.4, f32[732,12]{0,1:T(8,128)} %get-tuple-element.253), kind=kOutput, calls=%fused_computation.4.clone.1 | convolution fusion | flops 530700000 | bytes 478756 | tf_op jit(solution)/shard_map/while/body/eval_jaxpr/qkr,rh->hqk/dot_general | solution.py:79
  28.5 9.1 %fusion.86 = f32[8,12,25,200]{3,1,2,0:T(8,128)} fusion(f32[8,12,25,200]{3,1,2,0:T(8,128)} %get-tuple-element.246, s32[]{:T(128)S(6)} %copy.134, s32[25,200]{1,0:T(8,128)S(1)} %dynamic-slice_bitcast_fusion.4, f32[732,12]{0,1:T(8,128)} %get-tuple-element.253), kind=kOutput, calls=%fused_computation.4.clone.1 | convolution fusion | flops 530700000 | bytes 478756 | tf_op jit(solution)/shard_map/while/body/eval_jaxpr/qkr,rh->hqk/dot_general | solution.py:79
  38.5 9.2 %fusion.86 = f32[8,12,25,200]{3,1,2,0:T(8,128)} fusion(f32[8,12,25,200]{3,1,2,0:T(8,128)} %get-tuple-element.246, s32[]{:T(128)S(6)} %copy.134, s32[25,200]{1,0:T(8,128)S(1)} %dynamic-slice_bitcast_fusion.4, f32[732,12]{0,1:T(8,128)} %get-tuple-element.253), kind=kOutput, calls=%fused_computation.4.clone.1 | convolution fusion | flops 530700000 | bytes 478756 | tf_op jit(solution)/shard_map/while/body/eval_jaxpr/qkr,rh->hqk/dot_general | solution.py:79
  48.4 9.1 %fusion.86 = f32[8,12,25,200]{3,1,2,0:T(8,128)} fusion(f32[8,12,25,200]{3,1,2,0:T(8,128)} %get-tuple-element.246, s32[]{:T(128)S(6)} %copy.134, s32[25,200]{1,0:T(8,128)S(1)} %dynamic-slice_bitcast_fusion.4, f32[732,12]{0,1:T(8,128)} %get-tuple-element.253), kind=kOutput, calls=%fused_computation.4.clone.1 | convolution fusion | flops 530700000 | bytes 478756 | tf_op jit(solution)/shard_map/while/body/eval_jaxpr/qkr,rh->hqk/dot_general | solution.py:79
  58.3 9.1 %fusion.86 = f32[8,12,25,200]{3,1,2,0:T(8,128)} fusion(f32[8,12,25,200]{3,1,2,0:T(8,128)} %get-tuple-element.246, s32[]{:T(128)S(6)} %copy.134, s32[25,200]{1,0:T(8,128)S(1)} %dynamic-slice_bitcast_fusion.4, f32[732,12]{0,1:T(8,128)} %get-tuple-element.253), kind=kOutput, calls=%fused_computation.4.clone.1 | convolution fusion | flops 530700000 | bytes 478756 | tf_op jit(solution)/shard_map/while/body/eval_jaxpr/qkr,rh->hqk/dot_general | solution.py:79
  68.2 9.2 %fusion.86 = f32[8,12,25,200]{3,1,2,0:T(8,128)} fusion(f32[8,12,25,200]{3,1,2,0:T(8,128)} %get-tuple-element.246, s32[]{:T(128)S(6)} %copy.134, s32[25,200]{1,0:T(8,128)S(1)} %dynamic-slice_bitcast_fusion.4, f32[732,12]{0,1:T(8,128)} %get-tuple-element.253), kind=kOutput, calls=%fused_computation.4.clone.1 | convolution fusion | flops 530700000 | bytes 478756 | tf_op jit(solution)/shard_map/while/body/eval_jaxpr/qkr,rh->hqk/dot_general | solution.py:79
  78.1 9.2 %fusion.86 = f32[8,12,25,200]{3,1,2,0:T(8,128)} fusion(f32[8,12,25,200]{3,1,2,0:T(8,128)} %get-tuple-element.246, s32[]{:T(128)S(6)} %copy.134, s32[25,200]{1,0:T(8,128)S(1)} %dynamic-slice_bitcast_fusion.4, f32[732,12]{0,1:T(8,128)} %get-tuple-element.253), kind=kOutput, calls=%fused_computation.4.clone.1 | convolution fusion | flops 530700000 | bytes 478756 | tf_op jit(solution)/shard_map/while/body/eval_jaxpr/qkr,rh->hqk/dot_general | solution.py:79
  88.0 9.2 %fusion.86 = f32[8,12,25,200]{3,1,2,0:T(8,128)} fusion(f32[8,12,25,200]{3,1,2,0:T(8,128)} %get-tuple-element.246, s32[]{:T(128)S(6)} %copy.134, s32[25,200]{1,0:T(8,128)S(1)} %dynamic-slice_bitcast_fusion.4, f32[732,12]{0,1:T(8,128)} %get-tuple-element.253), kind=kOutput, calls=%fused_computation.4.clone.1 | convolution fusion | flops 530700000 | bytes 478756 | tf_op jit(solution)/shard_map/while/body/eval_jaxpr/qkr,rh->hqk/dot_general | solution.py:79
  97.2 4.7 copy.102
  102.6 8.1 add_convert_fusion
  110.7 14.9 %reshape.241 = bf16[5,200,3,12,64]{4,3,2,1,0:T(8,128)(2,1)} reshape(bf16[1000,2304]{1,0:T(8,128)(2,1)} %add_convert_fusion) | data formatting | bytes 9216000 | tf_op jit(solution)/shard_map/reshape | solution.py:157
  125.6 8.4 fusion.50
  134.0 6.0 copy.125
  140.0 6.0 copy.124
  146.0 6.2 copy.126
  152.2 6.2 fusion.52
  158.5 2.9 exponential_reduce_fusion
  165.5 3.1 copy.104
  168.6 5.8 convert_element_type.161
  174.4 6.4 multiply_add_fusion.2
  190.4 2.9 multiply_convert_fusion.4
  194.8 41.3 %all-gather.3.cloned.1.call-done = bf16[4000,768]{1,0:T(8,128)(2,1)} async-done(((bf16[1000,768]{1,0:T(8,128)(2,1)}), bf16[4000,768]{1,0:T(8,128)(2,1)}) %all-gather.3.cloned.1.call-update) | async-done | bytes 6144016 | tf_op jit(solution)/shard_map/all_gather | solution.py:179
  236.1 12.7 %multiply_convert_fusion.1 = (bf16[4000,768]{1,0:T(8,128)(2,1)}, f32[4000,768]{1,0:T(8,128)}) fusion(f32[768]{0:T(1024)} %dynamic_slice.14, bf16[4000,768]{1,0:T(8,128)(2,1)} %all-gather.3.cloned.1.call-done, bf16[768,768]{1,0:T(8,128)(2,1)} %param.39), kind=kOutput, calls=%fused_computation.26 | convolution fusion | flops 4737024000 | bytes 25758720 | tf_op jit(solution)/shard_map/dot_general | solution.py:181
  248.8 34.4 %all-gather.5.cloned.1.call-done = bf16[4000,768]{1,0:T(8,128)(2,1)} async-done(((bf16[1000,768]{1,0:T(8,128)(2,1)}), bf16[4000,768]{1,0:T(8,128)(2,1)}) %all-gather.5.cloned.1.call-update) | async-done | bytes 6144016 | tf_op jit(solution)/shard_map/all_gather | solution.py:200
  283.2 12.4 %convert_reduce_fusion.1 = (f32[768]{0:T(1024)}, bf16[4000,768]{1,0:T(8,128)(2,1)S(1)}) fusion(f32[4000,768]{1,0:T(8,128)} %get-tuple-element.182, f32[768]{0:T(1024)} %dynamic_slice.14, bf16[4000,768]{1,0:T(8,128)(2,1)} %all-gather.5.cloned.1.call-done, bf16[768,768]{1,0:T(8,128)(2,1)} %param.40), kind=kOutput, calls=%fused_computation.23 | convolution fusion | flops 4758526976 | bytes 25761792 | tf_op jit(solution)/shard_map/dot_general | solution.py:201
  298.3 7.9 fusion.54
  306.7 12.7 %convolution_convert_fusion = bf16[4000,768]{1,0:T(8,128)(2,1)} fusion(bf16[4000,768]{1,0:T(8,128)(2,1)} %get-tuple-element.181, bf16[768,768]{1,0:T(8,128)(2,1)} %param.40), kind=kOutput, calls=%fused_computation.36 | convolution fusion | flops 4721664000 | bytes 13467648 | tf_op jit(solution)/shard_map/dot_general | solution.py:185
  319.5 3.8 add_convert_fusion.1
  323.3 80.8 %reduce-scatter.7.cloned.1.call-done = f32[1000,768]{1,0:T(8,128)} async-done(((f32[4000,768]{1,0:T(8,128)}), f32[1000,768]{1,0:T(8,128)}) %reduce-scatter.7.cloned.1.call-update) | async-done | bytes 3072016 | tf_op jit(solution)/shard_map/reduce_scatter | solution.py:214
  404.1 4.2 multiply_reduce_fusion.3
  408.9 55.5 %reduce-scatter.5.cloned.1.call-done = bf16[1000,768]{1,0:T(8,128)(2,1)} async-done(((bf16[4000,768]{1,0:T(8,128)(2,1)}), bf16[1000,768]{1,0:T(8,128)(2,1)}) %reduce-scatter.5.cloned.1.call-update) | async-done | bytes 1536016 | tf_op jit(solution)/shard_map/reduce_scatter | solution.py:184
  464.4 8.4 multiply_reduce_fusion.2
  479.2 4.3 convolution_convert_fusion.2
  483.7 5.8 reshape.242
  489.5 6.1 copy.106
  495.5 13.1 %multiply_reduce_fusion = (f32[5,12,200]{2,1,0:T(8,128)S(1)}, f32[5,12,200,200]{2,3,1,0:T(8,128)}) fusion(f32[5,12,200,200]{2,3,1,0:T(8,128)} %copy-done.1, f32[5,12,200]{2,1,0:T(8,128)} %copy-done.9, bf16[5,200,12,64]{1,3,2,0:T(8,128)(2,1)} %copy.106, bf16[5,200,1,12,64]{1,4,3,0,2:T(8,128)(2,1)} %copy.124), kind=kOutput, calls=%fused_computation.25 | convolution fusion | flops 314388000 | bytes 22368000 | tf_op jit(solution)/shard_map/bqhd,bkhd->bhqk/dot_general | solution.py:238
  508.6 12.1 %convert_reduce_fusion = (f32[12,200,200]{1,2,0:T(8,128)}, bf16[5,12,200,200]{2,3,1,0:T(8,128)(2,1)S(1)}) fusion(f32[5,12,200,200]{2,3,1,0:T(8,128)} %get-tuple-element.184, f32[5,12,200]{2,1,0:T(8,128)S(1)} %get-tuple-element.183, f32[5,12,200,200]{2,3,1,0:T(8,128)} %copy-done.1, f32[5,12,200]{2,1,0:T(8,128)S(1)} %copy-done.10), kind=kLoop, calls=%fused_computation.22 | loop fusion | flops 13920000 | bytes 26016000 | tf_op jit(solution)/shard_map/reduce_sum | solution.py:251
  520.7 5.1 multiply_bitcast_fusion
  528.5 5.1 convolution_bitcast_fusion
  533.6 6.7 convert_reduce_fusion.2
  540.3 11.3 %copy.111 = bf16[5,200,3,12,64]{1,0,4,3,2:T(8,128)(2,1)} copy(bf16[5,200,3,12,64]{1,4,3,0,2:T(8,128)(2,1)} %get-tuple-element.165) | data formatting | bytes 9216000 | tf_op jit(solution)/shard_map/convert_element_type | solution.py:256
  551.6 13.8 %convert_element_type.177 = bf16[1000,2304]{0,1:T(8,128)(2,1)} reshape(bf16[5,200,3,12,64]{1,0,4,3,2:T(8,128)(2,1)} %copy.111) | data formatting | bytes 9216000 | tf_op jit(solution)/shard_map/convert_element_type | solution.py:256
  565.3 8.4 convolution_convert_fusion.1
  573.8 10.2 %convolution_convert_fusion.3 = bf16[768,768]{0,1:T(8,128)(2,1)} fusion(bf16[4000,768]{1,0:T(8,128)(2,1)} %all-gather.5.cloned.1.call-done, bf16[4000,768]{1,0:T(8,128)(2,1)} %get-tuple-element.181), kind=kOutput, calls=%fused_computation.79 | convolution fusion | flops 4719181824 | bytes 13467648 | tf_op jit(solution)/shard_map/dot_general | solution.py:202
  584.0 10.0 %convolution_convert_fusion.4 = bf16[768,768]{0,1:T(8,128)(2,1)} fusion(bf16[4000,768]{1,0:T(8,128)(2,1)} %all-gather.3.cloned.1.call-done, bf16[4000,768]{1,0:T(8,128)(2,1)} %copy-done.38), kind=kOutput, calls=%fused_computation.80 | convolution fusion | flops 4719181824 | bytes 13467648 | tf_op jit(solution)/shard_map/dot_general | solution.py:206
  594.0 20.4 %reduce-scatter.9.cloned.1.call-done = bf16[768,576]{0,1:T(8,128)(2,1)} async-done(((bf16[768,2304]{0,1:T(8,128)(2,1)}), bf16[768,576]{0,1:T(8,128)(2,1)}) %reduce-scatter.9.cloned.1.call-update) | async-done | bytes 884752 | tf_op jit(solution)/shard_map/reduce_scatter | solution.py:288
  614.3 3.5 pad_maximum_fusion
  617.8 5.8 copy.112
  623.6 5.6 all-to-all-start
  639.2 3.2 copy.113
  646.4 3.6 reshape.234
  650.0 10.1 %multiply_reduce_fusion.4 = (f32[768]{0:T(1024)S(1)}, f32[1000]{0:T(1024)}, f32[1000]{0:T(1024)}, f32[768]{0:T(1024)S(1)}, f32[1000,768]{1,0:T(8,128)}) fusion(f32[1000]{0:T(1024)} %rsqrt.21, f32[1000]{0:T(1024)} %div.123, bf16[5,200,768]{2,1,0:T(8,128)(2,1)} %param.33, f32[768]{0:T(1024)S(1)} %copy-done.28, bf16[1000,2304]{0,1:T(8,128)(2,1)} %convert_element_type.177, ...), kind=kOutput, calls=%fused_computation.45 | convolution fusion | flops 3548924416 | bytes 14316160 | tf_op jit(solution)/shard_map/dot_general | solution.py:262
  665.5 59.9 %while.22 = (s32[]{:T(128)}, f32[732,12]{0,1:T(8,128)}, s32[8,25,200]{2,1,0:T(8,128)}, f32[8,12,25,200]{3,2,0,1:T(8,128)}, s32[]{:T(128)}, /*index=5*/s32[]{:T(128)}) while((s32[]{:T(128)}, f32[732,12]{0,1:T(8,128)}, s32[8,25,200]{2,1,0:T(8,128)}, f32[8,12,25,200]{3,2,0,1:T(8,128)}, s32[]{:T(128)}, /*index=5*/s32[]{:T(128)}) %tuple.116), condition=%wide.region_39.40_spmd.clone, body=%wide.region_38.39_spmd.clone.sunk | while | flops 530717568 | bytes 850367 | solution.py:97
  667.2 5.0 fusion.87
  674.0 5.8 fusion.87
  681.6 5.8 fusion.87
  689.2 5.8 fusion.87
  696.8 5.8 fusion.87
  704.3 5.8 fusion.87
  711.9 5.8 fusion.87
  719.5 5.8 fusion.87
  733.5 5.9 multiply_add_fusion
  739.4 118.5 %all-reduce.4.cloned.1.call-done = (f32[32]{0:T(128)}, f32[10,768]{1,0:T(8,128)}, f32[3072]{0:T(1024)}, f32[732,12]{0,1:T(8,128)}) async-done(((f32[32]{0:T(128)}, f32[10,768]{1,0:T(8,128)}, f32[3072]{0:T(1024)}, f32[732,12]{0,1:T(8,128)}), (f32[32]{0:T(128)}, f32[10,768]{1,0:T(8,128)}, f32[3072]{0:T(1024)}, f32[732,12]{0,1:T(8,128)})) %all-reduce.4.cloned.1.call-update) | async-done | bytes 78288
  (186 shorter events, 100.3 us)
Async XLA Ops:
  7.2 95.4 %copy-start = (bf16[768,2304]{1,0:T(8,128)(2,1)S(1)}, bf16[768,2304]{1,0:T(8,128)(2,1)}, u32[]{:S(2)}) copy-start(bf16[768,2304]{1,0:T(8,128)(2,1)} %param.37) | copy-start | bytes 10616836
  7.2 228.9 %all-gather.3.cloned.1.call-start = ((), (), s32[]{:S(2)}) async-start(), calls=%async_computation.5 | async-start | bytes 7680000 | tf_op jit(solution)/shard_map/all_gather | solution.py:179
  13.7 4.2 copy-start.20
  97.2 5.4 copy-start.27
  97.2 5.4 copy-start.30
  146.0 6.2 copy-start.35
  158.4 4.8 copy-start.1
  158.5 4.8 copy-start.5
  163.2 2.2 copy-start.9
  168.6 5.8 copy-start.31
  168.6 5.8 copy-start.34
  182.9 3.1 copy-start.2
  182.9 3.1 copy-start.22
  182.9 3.1 copy-start.33
  185.4 0.6 copy-start.24
  186.0 4.4 copy-start.21
  187.7 95.5 %all-gather.5.cloned.1.call-start = ((), (), s32[]{:S(2)}) async-start(), calls=%async_computation.7 | async-start | bytes 7680000 | tf_op jit(solution)/shard_map/all_gather | solution.py:200
  193.4 210.7 %reduce-scatter.7.cloned.1.call-start = ((), (), s32[]{:S(2)}) async-start(), calls=%async_computation.8 | async-start | bytes 15360000 | tf_op jit(solution)/shard_map/reduce_scatter | solution.py:214
  283.2 15.1 %copy-start.37 = (bf16[768,768]{1,0:T(8,128)(2,1)S(1)}, bf16[768,768]{1,0:T(8,128)(2,1)}, u32[]{:S(2)}) copy-start(bf16[768,768]{1,0:T(8,128)(2,1)} %param.39) | copy-start | bytes 3538948
  295.7 2.7 copy-start.38
  306.3 158.1 %reduce-scatter.5.cloned.1.call-start = ((), (), s32[]{:S(2)}) async-start(), calls=%async_computation.6 | async-start | bytes 7680000 | tf_op jit(solution)/shard_map/reduce_scatter | solution.py:184
  319.4 274.5 %reduce-scatter.11.cloned.1.call-start = ((), (), s32[]{:S(2)}) async-start(), calls=%async_computation.10 | async-start | bytes 1474560 | tf_op jit(solution)/shard_map/reduce_scatter | solution.py:291
  323.3 141.2 %copy-start.23 = (f32[768]{0:T(1024)S(1)}, f32[768]{0:T(1024)}, u32[]{:S(2)}) copy-start(f32[768]{0:T(1024)} %get-tuple-element.105) | copy-start | bytes 9220
  323.3 141.2 %copy-start.25 = (f32[1000]{0:T(1024)S(1)}, f32[1000]{0:T(1024)}, u32[]{:S(2)}) copy-start(f32[1000]{0:T(1024)} %copy-done.24) | copy-start | bytes 12004
  464.4 10.0 %copy-start.32 = (f32[768]{0:T(1024)S(1)}, f32[768]{0:T(1024)}, u32[]{:S(2)}) copy-start(f32[768]{0:T(1024)} %get-tuple-element.111) | copy-start | bytes 9220
  472.8 1.6 copy-start.3
  472.8 3.9 copy-start.11
  475.5 1.2 copy-start.12
  483.5 130.9 %reduce-scatter.9.cloned.1.call-start = ((), (), s32[]{:S(2)}) async-start(), calls=%async_computation.9 | async-start | bytes 4423680 | tf_op jit(solution)/shard_map/reduce_scatter | solution.py:288
  495.5 13.1 %copy-start.10 = (f32[5,12,200]{2,1,0:T(8,128)S(1)}, f32[5,12,200]{2,1,0:T(8,128)}, u32[]{:S(2)}) copy-start(f32[5,12,200]{2,1,0:T(8,128)} %copy-done.9) | copy-start | bytes 144004
  508.6 19.9 %slice-start = ((s8[12288000]{0:T(1024)(128)(4,1)}), s8[4194304]{0:T(1024)(128)(4,1)S(1)}, s32[]{:S(2)}) async-start(s8[12288000]{0:T(1024)(128)(4,1)} %bitcast.123), calls=%async_computation.12 | async-start | bytes 8388608
  508.6 19.9 %slice-start.1 = ((s8[12288000]{0:T(1024)(128)(4,1)}), s8[4194304]{0:T(1024)(128)(4,1)S(1)}, s32[]{:S(2)}) async-start(s8[12288000]{0:T(1024)(128)(4,1)} %bitcast.123), calls=%async_computation.13 | async-start | bytes 8388608
  520.7 5.1 copy-start.4
  520.7 7.8 slice-start.2
  528.5 5.1 copy-start.8
  623.6 5.7 copy-start.19
  623.6 101.7 %all-to-all-start = ((bf16[8,96,2304]{2,1,0:T(8,128)(2,1)}), bf16[8,96,2304]{2,1,0:T(8,128)(2,1)}, u32[]{:S(2)}, u32[]{:S(2)}) async-start(bf16[8,96,2304]{2,1,0:T(8,128)(2,1)} %bitcast.127), calls=%async_computation.4 | async-start | bytes 7077888 | tf_op jit(solution)/shard_map/all_to_all | solution.py:30
  629.2 228.7 %all-reduce.4.cloned.1.call-start = ((), (), s32[]{:S(2)}) async-start(), calls=%async_computation.11 | async-start | bytes 222208
  632.8 17.2 %copy-start.26 = (f32[3072]{0:T(1024)}, f32[3072]{0:T(1024)S(1)}, u32[]{:S(2)}) copy-start(f32[3072]{0:T(1024)S(1)} %dynamic_update_slice.7) | copy-start | bytes 36868
  642.4 7.6 copy-start.28
  727.9 1.5 copy-start.6
  732.9 0.5 copy-start.36
  733.5 132.5 %copy-start.29 = (f32[3072]{0:T(1024)S(1)}, f32[3072]{0:T(1024)}, u32[]{:S(2)}) copy-start(f32[3072]{0:T(1024)} %param.42) | copy-start | bytes 36868
  865.9 8.9 %copy-start.7 = (f32[96,2304]{1,0:T(8,128)S(1)}, f32[96,2304]{1,0:T(8,128)}, u32[]{:S(2)}) copy-start(f32[96,2304]{1,0:T(8,128)} %copy-done.6) | copy-start | bytes 2654212
  866.0 8.9 %copy-start.13 = (f32[96,768]{1,0:T(8,128)S(1)}, f32[96,768]{1,0:T(8,128)}, u32[]{:S(2)}) copy-start(f32[96,768]{1,0:T(8,128)} %param.53) | copy-start | bytes 884740
  866.0 8.9 %copy-start.14 = (f32[96,768]{1,0:T(8,128)S(1)}, f32[96,768]{1,0:T(8,128)}, u32[]{:S(2)}) copy-start(f32[96,768]{1,0:T(8,128)} %param.55) | copy-start | bytes 884740
  866.0 8.9 %copy-start.15 = (f32[96,768]{1,0:T(8,128)S(1)}, f32[96,768]{1,0:T(8,128)}, u32[]{:S(2)}) copy-start(f32[96,768]{1,0:T(8,128)} %param.54) | copy-start | bytes 884740
  866.0 8.9 %copy-start.16 = (f32[96,768]{1,0:T(8,128)S(1)}, f32[96,768]{1,0:T(8,128)}, u32[]{:S(2)}) copy-start(f32[96,768]{1,0:T(8,128)} %param.50) | copy-start | bytes 884740
  866.0 8.9 %copy-start.17 = (f32[96,768]{1,0:T(8,128)S(1)}, f32[96,768]{1,0:T(8,128)}, u32[]{:S(2)}) copy-start(f32[96,768]{1,0:T(8,128)} %param.52) | copy-start | bytes 884740
  866.0 8.9 %copy-start.18 = (f32[96,768]{1,0:T(8,128)S(1)}, f32[96,768]{1,0:T(8,128)}, u32[]{:S(2)}) copy-start(f32[96,768]{1,0:T(8,128)} %param.51) | copy-start | bytes 884740
Sparse Core Ops, SparseCore 0:
  187.8 48.2 all-gather.2
  237.7 45.5 all-gather.4
  306.4 97.6 reduce-scatter.6
  406.5 57.8 reduce-scatter.4
  483.6 25.6 reduce-scatter.10
  573.9 40.3 reduce-scatter.8
  733.6 124.2 all-reduce.3
